TPU v7x, 128 devices: a whole 4x4x4 slice. The times are simulated.
128 devices in a mesh: gx: 16 (over y, x_hi, core), gy: 8 (over z, x_lo).
Axes of the slice: x: 4 (x_hi: 2, x_lo: 2; x = x_hi * 2 + x_lo), y: 4, z: 4, core: 2. Of those that a mesh axis runs over, the one named last changes fastest.
Arguments:
- forces: float32 [3, 24, 32, 64, 128], P(None, None, 'gx', 'gy'), may hold values from -6 to 6
- levels: int32 [32, 64, 128], P('gx', 'gy'), may hold values from 0 to 15
- supports: int32 [32, 64, 128], P('gx', 'gy'), may hold values 0 or 1
Outputs:
- filtered: float32 [32, 64, 128], P('gx', 'gy')
All inputs are finite; a program needn't handle non-finite values. No bound on the sum of `supports` on one device may be relied on, other than what follows from the above.
Results may differ from a plain program's by a relative error of at most 0.0001.
Values sent between devices are 32-bit elements; how exact they have to be, the bound alone decides.
A program may use at most 128 MiB of HBM per device.

v0:
```python
import math
import jax
import jax.numpy as jnp
import numpy as np
from jax import lax
from jax.sharding import PartitionSpec as P

CASES = 24
LEVELS = 16
ITERS = 2
load_factor = 0.2


def from_behind(value, axis, steps):
    count = lax.axis_size(axis)
    leading, last = (max(0, -steps), min(count, count - steps))
    return lax.ppermute(value, axis, [(source, source + steps) for source in range(leading, last)])


def extended_2(x, sides, width):
    for axis, dim in sides:
        count, length = (lax.axis_size(axis), x.shape[dim])
        up = [(i, (i + 1) % count) for i in range(count - 1)]
        down = [(j, i) for i, j in up]
        last = lax.slice_in_dim(x, length - width, length, axis=dim)
        leading = lax.slice_in_dim(x, 0, width, axis=dim)
        before = lax.ppermute(last, axis, up)
        after = lax.ppermute(leading, axis, down)
        x = jnp.concatenate([before, x, after], axis=dim)
    return x


def element_matrix():
    poisson = 0.3
    lame_first = poisson / ((1.0 + poisson) * (1.0 - 2.0 * poisson))
    lame_shear = 1.0 / (2.0 * (1.0 + poisson))
    elastic = np.zeros((6, 6))
    elastic[:3, :3] = lame_first
    for position in range(3):
        elastic[position, position] += 2.0 * lame_shear
        elastic[position + 3, position + 3] = lame_shear
    points = [0.5 - 0.5 / math.sqrt(3.0), 0.5 + 0.5 / math.sqrt(3.0)]
    matrix = np.zeros((24, 24))
    for point_x in points:
        for point_y in points:
            for point_z in points:
                coords = (point_x, point_y, point_z)
                strain = np.zeros((6, 24))
                for corner in range(8):
                    corner_bits = (corner >> 2 & 1, corner >> 1 & 1, corner & 1)
                    shape_values = [
                        coords[axis_n] if corner_bits[axis_n] else 1.0 - coords[axis_n]
                        for axis_n in range(3)
                    ]
                    slopes = [1.0 if corner_bits[axis_n] else -1.0 for axis_n in range(3)]
                    slope_x = slopes[0] * shape_values[1] * shape_values[2]
                    slope_y = shape_values[0] * slopes[1] * shape_values[2]
                    slope_z = shape_values[0] * shape_values[1] * slopes[2]
                    offset = 3 * corner
                    strain[0, offset] = slope_x
                    strain[1, offset + 1] = slope_y
                    strain[2, offset + 2] = slope_z
                    strain[3, offset] = slope_y
                    strain[3, offset + 1] = slope_x
                    strain[4, offset + 1] = slope_z
                    strain[4, offset + 2] = slope_y
                    strain[5, offset] = slope_z
                    strain[5, offset + 2] = slope_x
                matrix = matrix + strain.T @ elastic @ strain / 8.0
    return matrix


def corner_stack(field_in, lead_in, span_x, span_y, span_z):
    pieces = []
    for corner in range(8):
        step_x, step_y, step_z = (corner >> 2 & 1, corner >> 1 & 1, corner & 1)
        pieces.append(
            field_in[
                :,
                :,
                lead_in + step_x : lead_in + step_x + span_x,
                lead_in + step_y : lead_in + step_y + span_y,
                lead_in + step_z : lead_in + step_z + span_z,
            ]
        )
    stacked = jnp.stack(pieces, 0)
    return stacked.reshape((24,) + stacked.shape[2:])


def element_forces(extended, stiff_ext, element_stiff):
    span_x, span_y, span_z = (extended.shape[2] - 2, extended.shape[3] - 2, extended.shape[4] - 2)
    outputs = []
    for first_case in range(0, extended.shape[1], 6):
        case_group = extended[:, first_case : first_case + 6]
        gathered = corner_stack(case_group, 0, span_x + 1, span_y + 1, span_z + 1)
        product = (
            jnp.einsum("ab,bcxyz->acxyz", element_stiff, gathered, precision=lax.Precision.HIGHEST)
            * stiff_ext
        )
        product = product.reshape((8, 3) + product.shape[1:])
        summed = jnp.zeros((3, case_group.shape[1], span_x, span_y, span_z), jnp.float32)
        for corner in range(8):
            step_x, step_y, step_z = (corner >> 2 & 1, corner >> 1 & 1, corner & 1)
            summed = (
                summed
                + product[corner][
                    :,
                    :,
                    1 - step_x : 1 - step_x + span_x,
                    1 - step_y : 1 - step_y + span_y,
                    1 - step_z : 1 - step_z + span_z,
                ]
            )
        outputs.append(summed)
    return jnp.concatenate(outputs, 1)


def element_energy(extended, element_stiff):
    span_x, span_y, span_z = (extended.shape[2] - 2, extended.shape[3] - 2, extended.shape[4] - 2)
    summed = jnp.zeros((span_x, span_y, span_z), jnp.float32)
    for first_case in range(0, extended.shape[1], 6):
        case_group = extended[:, first_case : first_case + 6]
        gathered = corner_stack(case_group, 1, span_x, span_y, span_z)
        product = jnp.einsum(
            "ab,bcxyz->acxyz", element_stiff, gathered, precision=lax.Precision.HIGHEST
        )
        summed = summed + jnp.sum(gathered * product, axis=(0, 1))
    return summed


def node_diagonal(stiff_ext, free_mask, element_stiff):
    span_x, span_y, span_z = free_mask.shape
    parts = []
    for component in range(3):
        summed = jnp.zeros((span_x, span_y, span_z), jnp.float32)
        for corner in range(8):
            step_x, step_y, step_z = (corner >> 2 & 1, corner >> 1 & 1, corner & 1)
            summed = (
                summed
                + stiff_ext[
                    1 - step_x : 1 - step_x + span_x,
                    1 - step_y : 1 - step_y + span_y,
                    1 - step_z : 1 - step_z + span_z,
                ]
                * element_stiff[3 * corner + component, 3 * corner + component]
            )
        parts.append(summed)
    diagonal = jnp.stack(parts, 0)[:, None]
    return 1.0 / (free_mask * diagonal + (1.0 - free_mask))


def block_gram(first_field, second_field):
    return jnp.einsum("kcxyz,kdxyz->cd", first_field, second_field, precision=lax.Precision.HIGHEST)


def combine(field_in, mixing):
    return jnp.einsum("kcxyz,cd->kdxyz", field_in, mixing, precision=lax.Precision.HIGHEST)


def cone_filter(rimmed, density):
    span_x, span_y, span_z = density.shape
    numerator = jnp.zeros((span_x, span_y, span_z), jnp.float32)
    denominator = jnp.zeros((span_x, span_y, span_z), jnp.float32)
    for shift_x in range(-2, 3):
        for shift_y in range(-2, 3):
            for shift_z in range(-2, 3):
                weight = 2.5 - math.sqrt(shift_x * shift_x + shift_y * shift_y + shift_z * shift_z)
                if weight > 0.0:
                    window = rimmed[
                        :,
                        2 + shift_x : 2 + shift_x + span_x,
                        2 + shift_y : 2 + shift_y + span_y,
                        2 + shift_z : 2 + shift_z + span_z,
                    ]
                    numerator = numerator + weight * window[0]
                    denominator = denominator + weight * window[1]
    return numerator / (density * denominator)


def local(forces, levels, supports):
    element_stiff = jnp.asarray(element_matrix(), jnp.float32)
    free_mask = (1 - supports).astype(jnp.float32)
    density = 0.3 + 0.7 * levels.astype(jnp.float32) / (LEVELS - 1)
    stiffness = density**3
    below_x = from_behind(stiffness[-1:], "gx", 1)
    widened = jnp.concatenate([below_x, stiffness], 0)
    below_y = from_behind(widened[:, -1:], "gy", 1)
    widened = jnp.concatenate([below_y, widened], 1)
    stiff_ext = jnp.pad(widened, ((0, 0), (0, 0), (1, 0)))
    inverse = node_diagonal(stiff_ext, free_mask, element_stiff)
    load_field = load_factor * free_mask * forces
    solution = jnp.zeros_like(load_field)
    residual = load_field
    direction = inverse * residual
    kept_rims = []
    alphas_kept = []
    for iteration in range(ITERS):
        extended = extended_2(free_mask * direction, (("gx", 2), ("gy", 3)), 1)
        extended = jnp.pad(extended, ((0, 0), (0, 0), (0, 0), (0, 0), (1, 1)))
        applied = (
            free_mask * element_forces(extended, stiff_ext, element_stiff)
            + (1.0 - free_mask) * direction
        )
        image_field, extended = (applied, extended)
        kept_rims.append(extended)
        curvature, along_dir = lax.psum(
            (block_gram(direction, image_field), block_gram(direction, residual)), ("gx", "gy")
        )
        factor = jnp.linalg.cholesky(curvature)
        step_alpha = jax.scipy.linalg.cho_solve((factor, True), along_dir)
        alphas_kept.append(step_alpha)
        solution = solution + combine(direction, step_alpha)
        residual = residual - combine(image_field, step_alpha)
        if iteration + 1 < ITERS:
            scaled_res = inverse * residual
            coupling = lax.psum(block_gram(image_field, scaled_res), ("gx", "gy"))
            step_beta = -jax.scipy.linalg.cho_solve((factor, True), coupling)
            direction = scaled_res + combine(direction, step_beta)
    masked_sol = free_mask * solution
    above_x = from_behind(masked_sol[:, :, :1], "gx", -1)
    sol_wide = jnp.concatenate([masked_sol, above_x], 2)
    above_y = from_behind(sol_wide[:, :, :, :1], "gy", -1)
    sol_wide = jnp.concatenate([sol_wide, above_y], 3)
    sol_ext = jnp.pad(sol_wide, ((0, 0), (0, 0), (1, 0), (1, 0), (1, 1)))
    energy = element_energy(sol_ext, element_stiff)
    sensitivity = -3.0 * density**2 * energy / CASES
    stacked = jnp.stack([density * sensitivity, jnp.ones_like(density)], 0)
    rimmed = extended_2(stacked, (("gx", 1), ("gy", 2)), 2)
    rimmed = jnp.pad(rimmed, ((0, 0), (0, 0), (0, 0), (2, 2)))
    return cone_filter(rimmed, density)


def solution(mesh):
    return jax.shard_map(
        local,
        mesh=mesh,
        in_specs=(P(None, None, "gx", "gy", None), P("gx", "gy", None), P("gx", "gy", None)),
        out_specs=P("gx", "gy", None),
        check_vma=False,
    )
```

profile of v0, /device:TPU:8, one launch (start us, length us, event | category | flops | bytes accessed | tf_op | source)
XLA Modules:
  0.0 547.2 jit_solution(6883320357306443744)
XLA Ops:
  17.1 6.0 %collective-permute-start.3 = (f32[3,24,1,8,128]{4,0,3,2,1:T(4,128)S(1)}, f32[3,24,1,8,128]{4,0,3,2,1:T(4,128)S(1)}, u32[]{:S(2)}, u32[]{:S(2)}) collective-permute-start(f32[3,24,1,8,128]{4,0,3,2,1:T(4,128)S(1)} %get-tuple-element.102), channel_id=1, source_target_pairs={{8,0},{16,8},{24,16},{32,24},{40,32},{48,40},{56,48},{64,56},{72,6... | collective-permute-start | bytes 884744 | tf_op jit(solution)/shard_map/ppermute | solution.py:28
  36.6 7.4 %collective-permute-done.5 = f32[3,24,4,1,128]{4,0,3,2,1:T(4,128)S(1)} collective-permute-done((f32[3,24,4,1,128]{4,0,3,2,1:T(4,128)S(1)}, f32[3,24,4,1,128]{4,0,3,2,1:T(4,128)S(1)}, u32[]{:S(2)}, u32[]{:S(2)}) %collective-permute-start.5) | collective-permute-done | bytes 147488 | tf_op jit(solution)/shard_map/ppermute | solution.py:28
  67.9 7.6 %reshape.547 = f32[24,6,3,9,129]{4,0,3,2,1:T(8,128)} reshape(f32[8,3,6,3,9,129]{5,1,0,4,3,2:T(4,128)} %copy.32) | data formatting | bytes 4012416 | tf_op jit(solution)/shard_map/reshape | solution.py:87
  77.8 6.4 %copy.35 = f32[8,3,6,3,9,129]{5,1,0,4,3,2:T(4,128)} copy(f32[8,3,6,3,9,129]{5,1,4,3,2,0:T(4,128)} %fusion.46) | data formatting | bytes 4012416 | tf_op jit(solution)/shard_map/stack | solution.py:86
  84.2 7.4 %reshape.550 = f32[24,6,3,9,129]{4,0,3,2,1:T(8,128)} reshape(f32[8,3,6,3,9,129]{5,1,0,4,3,2:T(4,128)} %copy.35) | data formatting | bytes 4012416 | tf_op jit(solution)/shard_map/reshape | solution.py:87
  91.7 7.8 %multiply_bitcast_fusion.7 = f32[24,6,3,9,129]{4,0,3,2,1:T(8,128)} fusion(f32[24,6,3,9,129]{4,0,3,2,1:T(8,128)} %reshape.547, f32[24,24,1,1,1]{1,0,4,3,2:T(8,128)S(1)} %copy-done.11, f32[3,9,129]{2,1,0:T(8,128)S(1)} %pad.20), kind=kOutput, calls=%fused_computation.25 | convolution fusion | flops 144948528 | bytes 4028652 | tf_op jit(solution)/shard_map/ab,bcxyz->acxyz/dot_general | solution.py:97
  108.4 7.7 %reshape.549 = f32[24,6,3,9,129]{4,0,3,2,1:T(8,128)} reshape(f32[8,3,6,3,9,129]{5,1,0,4,3,2:T(4,128)} %copy.34) | data formatting | bytes 4012416 | tf_op jit(solution)/shard_map/reshape | solution.py:87
  116.1 7.6 %multiply_bitcast_fusion.5 = f32[24,6,3,9,129]{4,0,3,2,1:T(8,128)} fusion(f32[24,6,3,9,129]{4,0,3,2,1:T(8,128)} %reshape.549, f32[24,24,1,1,1]{1,0,4,3,2:T(8,128)S(1)} %copy-done.11, f32[3,9,129]{2,1,0:T(8,128)S(1)} %pad.20), kind=kOutput, calls=%fused_computation.23 | convolution fusion | flops 144948528 | bytes 4028652 | tf_op jit(solution)/shard_map/ab,bcxyz->acxyz/dot_general | solution.py:97
  123.7 6.5 %copy.33 = f32[8,3,6,3,9,129]{5,1,0,4,3,2:T(4,128)} copy(f32[8,3,6,3,9,129]{5,1,4,3,2,0:T(4,128)} %copy-done.6) | data formatting | bytes 4012416 | tf_op jit(solution)/shard_map/stack | solution.py:86
  130.2 7.4 %reshape.548 = f32[24,6,3,9,129]{4,0,3,2,1:T(8,128)} reshape(f32[8,3,6,3,9,129]{5,1,0,4,3,2:T(4,128)} %copy.33) | data formatting | bytes 4012416 | tf_op jit(solution)/shard_map/reshape | solution.py:87
  142.9 5.7 %slice_add_fusion.28 = (f32[3,6,2,8,128]{4,0,3,2,1:T(4,128)S(1)}, f32[3,6,2,8,128]{4,0,3,2,1:T(4,128)S(1)}) fusion(f32[24,6,3,9,129]{4,0,3,2,1:T(8,128)} %multiply_bitcast_fusion.4, f32[24,6,3,9,129]{4,0,3,2,1:T(8,128)} %multiply_bitcast_fusion.5), kind=kLoop, calls=%fused_computation.312 | loop fusion | flops 516096 | bytes 2654208 | tf_op jit(solution)/shard_map/add | solution.py:105
  156.1 67.5 %all-reduce.7 = (f32[24,24]{1,0:T(8,128)S(1)}, f32[24,24]{0,1:T(8,128)S(1)}) all-reduce(f32[24,24]{1,0:T(8,128)S(1)} %convolution_bitcast_fusion.5, f32[24,24]{0,1:T(8,128)S(1)} %convolution_bitcast_fusion.6), channel_id=1, replica_groups=mesh['gx'=16,'gy'=8] {'gx','gy'}, use_global_device_ids=true, to_apply=%region_3.5 | all-reduce | flops 1152 | bytes 9216 | tf_op jit(solution)/shard_map/psum | solution.py:206
  233.4 62.4 %psum.37 = f32[24,24]{1,0:T(8,128)S(1)} all-reduce(f32[24,24]{1,0:T(8,128)S(1)} %convolution_bitcast_fusion.3), channel_id=1, replica_groups=mesh['gx'=16,'gy'=8] {'gx','gy'}, use_global_device_ids=true, to_apply=%region_4.7 | all-reduce | flops 576 | bytes 4608 | tf_op jit(solution)/shard_map/psum | solution.py:216
  300.2 6.0 %collective-permute-start.7 = (f32[3,24,1,8,128]{4,0,3,2,1:T(4,128)S(1)}, f32[3,24,1,8,128]{4,0,3,2,1:T(4,128)S(1)}, u32[]{:S(2)}, u32[]{:S(2)}) collective-permute-start(f32[3,24,1,8,128]{4,0,3,2,1:T(4,128)S(1)} %get-tuple-element.100), channel_id=1, source_target_pairs={{8,0},{16,8},{24,16},{32,24},{40,32},{48,40},{56,48},{64,56},{72,6... | collective-permute-start | bytes 884744 | tf_op jit(solution)/shard_map/ppermute | solution.py:28
  319.2 7.2 %collective-permute-done.9 = f32[3,24,4,1,128]{4,0,3,2,1:T(4,128)S(1)} collective-permute-done((f32[3,24,4,1,128]{4,0,3,2,1:T(4,128)S(1)}, f32[3,24,4,1,128]{4,0,3,2,1:T(4,128)S(1)}, u32[]{:S(2)}, u32[]{:S(2)}) %collective-permute-start.9) | collective-permute-done | bytes 147488 | tf_op jit(solution)/shard_map/ppermute | solution.py:28
  350.3 7.4 %reshape.551 = f32[24,6,3,9,129]{4,0,3,2,1:T(8,128)} reshape(f32[8,3,6,3,9,129]{5,1,0,4,3,2:T(4,128)} %copy.47) | data formatting | bytes 4012416 | tf_op jit(solution)/shard_map/reshape | solution.py:87
  366.0 6.4 %copy.50 = f32[8,3,6,3,9,129]{5,1,0,4,3,2:T(4,128)} copy(f32[8,3,6,3,9,129]{5,1,4,3,2,0:T(4,128)} %fusion.14) | data formatting | bytes 4012416 | tf_op jit(solution)/shard_map/stack | solution.py:86
  372.4 7.4 %reshape.554 = f32[24,6,3,9,129]{4,0,3,2,1:T(8,128)} reshape(f32[8,3,6,3,9,129]{5,1,0,4,3,2:T(4,128)} %copy.50) | data formatting | bytes 4012416 | tf_op jit(solution)/shard_map/reshape | solution.py:87
  385.6 6.4 %copy.49 = f32[8,3,6,3,9,129]{5,1,0,4,3,2:T(4,128)} copy(f32[8,3,6,3,9,129]{5,1,4,3,2,0:T(4,128)} %copy-done.7) | data formatting | bytes 4012416 | tf_op jit(solution)/shard_map/stack | solution.py:86
  392.0 7.4 %reshape.553 = f32[24,6,3,9,129]{4,0,3,2,1:T(8,128)} reshape(f32[8,3,6,3,9,129]{5,1,0,4,3,2:T(4,128)} %copy.49) | data formatting | bytes 4012416 | tf_op jit(solution)/shard_map/reshape | solution.py:87
  405.1 6.5 %copy.48 = f32[8,3,6,3,9,129]{5,1,0,4,3,2:T(4,128)} copy(f32[8,3,6,3,9,129]{5,1,4,3,2,0:T(4,128)} %copy-done.8) | data formatting | bytes 4012416 | tf_op jit(solution)/shard_map/stack | solution.py:86
  411.6 7.6 %reshape.552 = f32[24,6,3,9,129]{4,0,3,2,1:T(8,128)} reshape(f32[8,3,6,3,9,129]{5,1,0,4,3,2:T(4,128)} %copy.48) | data formatting | bytes 4012416 | tf_op jit(solution)/shard_map/reshape | solution.py:87
  426.6 64.6 %all-reduce.6 = (f32[24,24]{1,0:T(8,128)S(1)}, f32[24,24]{0,1:T(8,128)S(1)}) all-reduce(f32[24,24]{1,0:T(8,128)S(1)} %convolution_bitcast_fusion.1, f32[24,24]{0,1:T(8,128)S(1)} %convolution_bitcast_fusion.2), channel_id=1, replica_groups=mesh['gx'=16,'gy'=8] {'gx','gy'}, use_global_device_ids=true, to_apply=%region_6.9 | all-reduce | flops 1152 | bytes 9216 | tf_op jit(solution)/shard_map/psum | solution.py:206
  507.3 5.9 %collective-permute-done.11 = f32[3,24,3,1,128]{4,1,3,2,0:T(8,128)S(1)} collective-permute-done((f32[3,24,3,1,128]{4,1,3,2,0:T(8,128)S(1)}, f32[3,24,3,1,128]{4,1,3,2,0:T(8,128)S(1)}, u32[]{:S(2)}, u32[]{:S(2)}) %collective-permute-start.11) | collective-permute-done | bytes 110624 | tf_op jit(solution)/shard_map/ppermute | solution.py:17
  (168 shorter events, 205.7 us)
Async XLA Ops:
  0.7 7.3 %collective-permute-start = (f32[1,8,128]{2,1,0:T(8,128)S(1)}, f32[1,8,128]{2,1,0:T(8,128)S(1)}, u32[]{:S(2)}, u32[]{:S(2)}) collective-permute-start(f32[1,8,128]{2,1,0:T(8,128)S(1)} %slice.2141), channel_id=1, source_target_pairs={{0,8},{8,16},{16,24},{24,32},{32,40},{40,48},{48,56},{56,64},{64,7... | collective-permute-start | bytes 12296 | tf_op jit(solution)/shard_map/ppermute | solution.py:17
  8.0 4.7 collective-permute-start.1
  15.1 12.7 %collective-permute-start.2 = (f32[3,24,1,8,128]{4,0,3,2,1:T(4,128)S(1)}, f32[3,24,1,8,128]{4,0,3,2,1:T(4,128)S(1)}, u32[]{:S(2)}, u32[]{:S(2)}) collective-permute-start(f32[3,24,1,8,128]{4,0,3,2,1:T(4,128)S(1)} %get-tuple-element.101), channel_id=1, source_target_pairs={{0,8},{8,16},{16,24},{24,32},{32,40},{40,48},{48,56},{56,64},{64,7... | collective-permute-start | bytes 884744 | tf_op jit(solution)/shard_map/ppermute | solution.py:27
  17.1 11.3 %collective-permute-start.3 = (f32[3,24,1,8,128]{4,0,3,2,1:T(4,128)S(1)}, f32[3,24,1,8,128]{4,0,3,2,1:T(4,128)S(1)}, u32[]{:S(2)}, u32[]{:S(2)}) collective-permute-start(f32[3,24,1,8,128]{4,0,3,2,1:T(4,128)S(1)} %get-tuple-element.102), channel_id=1, source_target_pairs={{8,0},{16,8},{24,16},{32,24},{40,32},{48,40},{56,48},{64,56},{72,6... | collective-permute-start | bytes 884744 | tf_op jit(solution)/shard_map/ppermute | solution.py:28
  28.5 8.1 %collective-permute-start.4 = (f32[3,24,4,1,128]{4,0,3,2,1:T(4,128)S(1)}, f32[3,24,4,1,128]{4,0,3,2,1:T(4,128)S(1)}, u32[]{:S(2)}, u32[]{:S(2)}) collective-permute-start(f32[3,24,4,1,128]{4,0,3,2,1:T(4,128)S(1)} %get-tuple-element.79), channel_id=1, source_target_pairs={{0,1},{1,2},{2,3},{3,4},{4,5},{5,6},{6,7},{8,9},{9,10},{10,11},{11... | collective-permute-start | bytes 442376 | tf_op jit(solution)/shard_map/ppermute | solution.py:27
  32.7 11.3 %collective-permute-start.5 = (f32[3,24,4,1,128]{4,0,3,2,1:T(4,128)S(1)}, f32[3,24,4,1,128]{4,0,3,2,1:T(4,128)S(1)}, u32[]{:S(2)}, u32[]{:S(2)}) collective-permute-start(f32[3,24,4,1,128]{4,0,3,2,1:T(4,128)S(1)} %get-tuple-element.80), channel_id=1, source_target_pairs={{1,0},{2,1},{3,2},{4,3},{5,4},{6,5},{7,6},{9,8},{10,9},{11,10},{12... | collective-permute-start | bytes 442376 | tf_op jit(solution)/shard_map/ppermute | solution.py:28
  48.2 7.3 %copy-start.1 = (f32[3,24,4,10,130]{4,0,3,2,1:T(4,128)}, f32[3,24,4,10,130]{4,0,3,2,1:T(4,128)S(1)}, u32[]{:S(2)}) copy-start(f32[3,24,4,10,130]{4,0,3,2,1:T(4,128)S(1)} %select_maximum_fusion.4) | copy-start | bytes 4492804
  84.2 7.4 %copy-start.11 = (f32[24,24,1,1,1]{1,0,4,3,2:T(8,128)S(1)}, f32[24,24,1,1,1]{1,0,4,3,2:T(8,128)}, u32[]{:S(2)}) copy-start(f32[24,24,1,1,1]{1,0,4,3,2:T(8,128)} %constant.139) | copy-start | bytes 6916
  91.6 7.8 %copy-start.2 = (f32[24,6,3,9,129]{4,0,3,2,1:T(8,128)S(1)}, f32[24,6,3,9,129]{4,0,3,2,1:T(8,128)}, u32[]{:S(2)}) copy-start(f32[24,6,3,9,129]{4,0,3,2,1:T(8,128)} %reshape.550) | copy-start | bytes 6018628
  91.6 12.8 %slice-start = ((s8[5308416]{0:T(1024)(128)(4,1)}), s8[4194304]{0:T(1024)(128)(4,1)S(1)}, s32[]{:S(2)}) async-start(s8[5308416]{0:T(1024)(128)(4,1)} %bitcast.1302), calls=%async_computation | async-start | bytes 8388608
  142.9 9.7 %copy-start.9 = (f32[3,24,2,8,128]{4,3,2,1,0:T(8,128)S(1)}, f32[3,24,2,8,128]{4,3,2,1,0:T(8,128)}, u32[]{:S(2)}) copy-start(f32[3,24,2,8,128]{4,3,2,1,0:T(8,128)} %param.7) | copy-start | bytes 1769476
  297.1 19.0 %copy-start.10 = (f32[3,24,2,8,128]{4,0,3,2,1:T(4,128)S(1)}, f32[3,24,2,8,128]{4,0,3,2,1:T(4,128)}, u32[]{:S(2)}) copy-start(f32[3,24,2,8,128]{4,0,3,2,1:T(4,128)} %get-tuple-element.14) | copy-start | bytes 1769476
  297.9 11.9 %collective-permute-start.6 = (f32[3,24,1,8,128]{4,0,3,2,1:T(4,128)S(1)}, f32[3,24,1,8,128]{4,0,3,2,1:T(4,128)S(1)}, u32[]{:S(2)}, u32[]{:S(2)}) collective-permute-start(f32[3,24,1,8,128]{4,0,3,2,1:T(4,128)S(1)} %get-tuple-element.99), channel_id=1, source_target_pairs={{0,8},{8,16},{16,24},{24,32},{32,40},{40,48},{48,56},{56,64},{64,7... | collective-permute-start | bytes 884744 | tf_op jit(solution)/shard_map/ppermute | solution.py:27
  300.2 11.3 %collective-permute-start.7 = (f32[3,24,1,8,128]{4,0,3,2,1:T(4,128)S(1)}, f32[3,24,1,8,128]{4,0,3,2,1:T(4,128)S(1)}, u32[]{:S(2)}, u32[]{:S(2)}) collective-permute-start(f32[3,24,1,8,128]{4,0,3,2,1:T(4,128)S(1)} %get-tuple-element.100), channel_id=1, source_target_pairs={{8,0},{16,8},{24,16},{32,24},{40,32},{48,40},{56,48},{64,56},{72,6... | collective-permute-start | bytes 884744 | tf_op jit(solution)/shard_map/ppermute | solution.py:28
  311.7 7.5 %collective-permute-start.8 = (f32[3,24,4,1,128]{4,0,3,2,1:T(4,128)S(1)}, f32[3,24,4,1,128]{4,0,3,2,1:T(4,128)S(1)}, u32[]{:S(2)}, u32[]{:S(2)}) collective-permute-start(f32[3,24,4,1,128]{4,0,3,2,1:T(4,128)S(1)} %get-tuple-element.77), channel_id=1, source_target_pairs={{0,1},{1,2},{2,3},{3,4},{4,5},{5,6},{6,7},{8,9},{9,10},{10,11},{11... | collective-permute-start | bytes 442376 | tf_op jit(solution)/shard_map/ppermute | solution.py:27
  314.8 11.6 %collective-permute-start.9 = (f32[3,24,4,1,128]{4,0,3,2,1:T(4,128)S(1)}, f32[3,24,4,1,128]{4,0,3,2,1:T(4,128)S(1)}, u32[]{:S(2)}, u32[]{:S(2)}) collective-permute-start(f32[3,24,4,1,128]{4,0,3,2,1:T(4,128)S(1)} %get-tuple-element.78), channel_id=1, source_target_pairs={{1,0},{2,1},{3,2},{4,3},{5,4},{6,5},{7,6},{9,8},{10,9},{11,10},{12... | collective-permute-start | bytes 442376 | tf_op jit(solution)/shard_map/ppermute | solution.py:28
  330.6 7.3 %copy-start = (f32[3,24,4,10,130]{4,0,3,2,1:T(4,128)}, f32[3,24,4,10,130]{4,0,3,2,1:T(4,128)S(1)}, u32[]{:S(2)}) copy-start(f32[3,24,4,10,130]{4,0,3,2,1:T(4,128)S(1)} %select_maximum_fusion) | copy-start | bytes 4492804
  498.1 7.6 %collective-permute-start.10 = (f32[3,24,1,8,128]{4,1,3,2,0:T(8,128)S(1)}, f32[3,24,1,8,128]{4,1,3,2,0:T(8,128)S(1)}, u32[]{:S(2)}, u32[]{:S(2)}) collective-permute-start(f32[3,24,1,8,128]{4,1,3,2,0:T(8,128)S(1)} %slice.2277), channel_id=1, source_target_pairs={{8,0},{16,8},{24,16},{32,24},{40,32},{48,40},{56,48},{64,56},{72,6... | collective-permute-start | bytes 884744 | tf_op jit(solution)/shard_map/ppermute | solution.py:17
  505.8 7.5 %collective-permute-start.11 = (f32[3,24,3,1,128]{4,1,3,2,0:T(8,128)S(1)}, f32[3,24,3,1,128]{4,1,3,2,0:T(8,128)S(1)}, u32[]{:S(2)}, u32[]{:S(2)}) collective-permute-start(f32[3,24,3,1,128]{4,1,3,2,0:T(8,128)S(1)} %pad_maximum_fusion.8), channel_id=1, source_target_pairs={{1,0},{2,1},{3,2},{4,3},{5,4},{6,5},{7,6},{9,8},{10,9},{11,10},{12... | collective-permute-start | bytes 331784 | tf_op jit(solution)/shard_map/ppermute | solution.py:17
  519.2 5.1 copy-start.12
  524.4 6.2 %collective-permute-start.13 = (f32[2,2,8,128]{3,2,1,0:T(8,128)S(1)}, f32[2,2,8,128]{3,2,1,0:T(8,128)S(1)}, u32[]{:S(2)}, u32[]{:S(2)}) collective-permute-start(f32[2,2,8,128]{3,2,1,0:T(8,128)S(1)} %stack.455), channel_id=1, source_target_pairs={{8,0},{16,8},{24,16},{32,24},{40,32},{48,40},{56,48},{64,56},{72,6... | collective-permute-start | bytes 49160 | tf_op jit(solution)/shard_map/ppermute | solution.py:28
  528.7 7.5 %collective-permute-start.12 = (f32[2,2,8,128]{3,2,1,0:T(8,128)S(1)}, f32[2,2,8,128]{3,2,1,0:T(8,128)S(1)}, u32[]{:S(2)}, u32[]{:S(2)}) collective-permute-start(f32[2,2,8,128]{3,2,1,0:T(8,128)S(1)} %stack.455), channel_id=1, source_target_pairs={{0,8},{8,16},{16,24},{24,32},{32,40},{40,48},{48,56},{56,64},{64,7... | collective-permute-start | bytes 49160 | tf_op jit(solution)/shard_map/ppermute | solution.py:27
  536.1 5.3 collective-permute-start.14
  540.1 5.6 %collective-permute-start.15 = (f32[2,6,2,128]{3,2,1,0:T(2,128)S(1)}, f32[2,6,2,128]{3,2,1,0:T(2,128)S(1)}, u32[]{:S(2)}, u32[]{:S(2)}) collective-permute-start(f32[2,6,2,128]{3,2,1,0:T(2,128)S(1)} %get-tuple-element.113), channel_id=1, source_target_pairs={{1,0},{2,1},{3,2},{4,3},{5,4},{6,5},{7,6},{9,8},{10,9},{11,10},{12... | collective-permute-start | bytes 36872 | tf_op jit(solution)/shard_map/ppermute | solution.py:28
  (7 other events, 19.1 us)
where the time goes:
time: 558 us; the launch traced here: 547 us
  blocking collectives  195 us (35%)
  local copies, waits for them, and re-layouts  142 us (25%)
  matrix products  67.7 us (12%)
  waiting for transfers between devices  54.4 us (10%)
  starting transfers between devices  47.9 us (9%)
  other arithmetic  39.2 us (7%)
    psum x2, blocking collectives, local(): lax.psum((block_gram(direction, image_field), block_gram(direction, resid...  132 us
    psum x1, blocking collectives, local(): coupling = lax.psum(block_gram(image_field, scaled_res), ('gx', 'gy'))  62.4 us
    reshape x8, local copies, waits for them, and re-layouts, corner_stack(): return stacked.reshape((24,) + stacked.shape[2:])  59.9 us
    another operation x16, local copies, waits for them, and re-layouts, corner_stack(): stacked = jnp.stack(pieces, 0)  52.4 us
    dot_general x8, matrix products, element_forces(): jnp.einsum('ab,bcxyz->acxyz', element_stiff, gathered, precision=lax.Prec...  46.9 us
    unnamed x55, local copies, waits for them, and re-layouts  29.4 us
    ppermute x6, waiting for transfers between devices, extended_2(): after = lax.ppermute(leading, axis, down)  21.1 us
    ppermute x6, starting transfers between devices, extended_2(): after = lax.ppermute(leading, axis, down)  20.2 us
  transfers between devices with their start and end apart: 16, of which 15 were waited for; matrix products, arithmetic and copies ran while one was open for 1% of the time, Pallas kernels for 0%

commit v1 on v0

--- a/solution.py
+++ b/solution.py
@@ -213,7 +213,9 @@
         residual = residual - combine(image_field, step_alpha)
         if iteration + 1 < ITERS:
             scaled_res = inverse * residual
-            coupling = lax.psum(block_gram(image_field, scaled_res), ("gx", "gy"))
+            coupling = jnp.sum(
+                lax.all_gather(block_gram(image_field, scaled_res), ("gx", "gy")), axis=0
+            )
             step_beta = -jax.scipy.linalg.cho_solve((factor, True), coupling)
             direction = scaled_res + combine(direction, step_beta)
     masked_sol = free_mask * solution

time: 558 us -> 806 us (1.44)
  blocking collectives: 195 us -> 443 us
    all_gather x0 -> x1, blocking collectives: none -> 282 us  [local(): lax.all_gather(block_gram(image_field, scaled_res), ('gx', 'gy'))]
    psum x1 -> x0, blocking collectives: 62.4 us -> none  [local(): coupling = lax.psum(block_gram(image_field, scaled_res), ('gx', 'gy'))]
    psum x2, blocking collectives: 132 us -> 161 us  [local(): lax.psum((block_gram(direction, image_field), block_gram(direction, resid...]
    unnamed x55 -> x57, local copies, waits for them, and re-layouts: 29.4 us -> 29.4 us
  transfers between devices with their start and end apart: 16 -> 16, of which waited for: 15 -> 15; matrix products, arithmetic and copies ran while one was open for 1% -> 0% of each run, Pallas kernels for 0% -> 0%
where the time goes in v1:
time: 806 us; the launch traced here: 795 us
  blocking collectives  443 us (55%)
  local copies, waits for them, and re-layouts  142 us (18%)
  matrix products  67.7 us (8%)
  waiting for transfers between devices  50.6 us (6%)
  starting transfers between devices  50 us (6%)
  other arithmetic  40.3 us (5%)
    all_gather x1, blocking collectives, local(): lax.all_gather(block_gram(image_field, scaled_res), ('gx', 'gy'))  282 us
    psum x2, blocking collectives, local(): lax.psum((block_gram(direction, image_field), block_gram(direction, resid...  161 us
    reshape x8, local copies, waits for them, and re-layouts, corner_stack(): return stacked.reshape((24,) + stacked.shape[2:])  59.8 us
    another operation x16, local copies, waits for them, and re-layouts, corner_stack(): stacked = jnp.stack(pieces, 0)  52.3 us
    dot_general x8, matrix products, element_forces(): jnp.einsum('ab,bcxyz->acxyz', element_stiff, gathered, precision=lax.Prec...  46.9 us
    unnamed x57, local copies, waits for them, and re-layouts  29.4 us
    ppermute x6, starting transfers between devices, extended_2(): after = lax.ppermute(leading, axis, down)  22 us
    ppermute x6, waiting for transfers between devices, extended_2(): after = lax.ppermute(leading, axis, down)  19.4 us
  transfers between devices with their start and end apart: 16, of which 15 were waited for; matrix products, arithmetic and copies ran while one was open for 0% of the time, Pallas kernels for 0%

profile of v1, /device:TPU:8, one launch (start us, length us, event | category | flops | bytes accessed | tf_op | source)
XLA Modules:
  0.0 795.0 jit_solution(10863054144200587620)
XLA Ops:
  17.1 6.0 collective-permute-start.3
  36.6 7.4 collective-permute-done.5
  67.8 7.6 reshape.547
  77.8 6.4 copy.37
  84.2 7.4 reshape.550
  91.6 7.8 multiply_bitcast_fusion.7
  108.4 7.7 reshape.549
  116.1 7.6 multiply_bitcast_fusion.5
  123.7 6.5 copy.35
  130.2 7.4 reshape.548
  142.9 5.5 slice_add_fusion.28
  155.7 67.5 %all-reduce.7 = (f32[24,24]{1,0:T(8,128)S(1)}, f32[24,24]{0,1:T(8,128)S(1)}) all-reduce(f32[24,24]{1,0:T(8,128)S(1)} %convolution_bitcast_fusion.5, f32[24,24]{0,1:T(8,128)S(1)} %convolution_bitcast_fusion.6), channel_id=1, replica_groups=mesh['gx'=16,'gy'=8] {'gx','gy'}, use_global_device_ids=true, to_apply=%region_3.5 | all-reduce | flops 1152 | bytes 9216 | tf_op jit(solution)/shard_map/psum | solution.py:206
  233.1 281.8 %all-gather = f32[3072,24]{1,0:T(8,128)S(1)} all-gather(f32[24,24]{1,0:T(8,128)S(1)} %convolution_bitcast_fusion.3), channel_id=2, replica_groups=mesh['gx'=16,'gy'=8] {'gx','gy'}, dimensions={0}, use_global_device_ids=true | all-gather | bytes 297216 | tf_op jit(solution)/shard_map/all_gather | solution.py:217
  520.2 6.0 collective-permute-start.7
  568.5 7.4 reshape.551
  584.2 6.4 copy.54
  590.6 7.4 reshape.554
  603.8 6.4 copy.53
  610.2 7.4 reshape.553
  623.3 6.5 copy.52
  629.8 7.6 reshape.552
  644.8 93.8 %all-reduce.6 = (f32[24,24]{1,0:T(8,128)S(1)}, f32[24,24]{0,1:T(8,128)S(1)}) all-reduce(f32[24,24]{1,0:T(8,128)S(1)} %convolution_bitcast_fusion.1, f32[24,24]{0,1:T(8,128)S(1)} %convolution_bitcast_fusion.2), channel_id=1, replica_groups=mesh['gx'=16,'gy'=8] {'gx','gy'}, use_global_device_ids=true, to_apply=%region_6.9 | all-reduce | flops 1152 | bytes 9216 | tf_op jit(solution)/shard_map/psum | solution.py:206
  770.8 5.7 collective-permute-start.13
  778.4 5.5 collective-permute-done.12
  (171 shorter events, 207.1 us)
Async XLA Ops:
  0.7 7.3 collective-permute-start
  8.0 4.7 collective-permute-start.1
  15.1 12.7 %collective-permute-start.2 = (f32[3,24,1,8,128]{4,0,3,2,1:T(4,128)S(1)}, f32[3,24,1,8,128]{4,0,3,2,1:T(4,128)S(1)}, u32[]{:S(2)}, u32[]{:S(2)}) collective-permute-start(f32[3,24,1,8,128]{4,0,3,2,1:T(4,128)S(1)} %get-tuple-element.101), channel_id=1, source_target_pairs={{0,8},{8,16},{16,24},{24,32},{32,40},{40,48},{48,56},{56,64},{64,7... | collective-permute-start | bytes 884744 | tf_op jit(solution)/shard_map/ppermute | solution.py:27
  17.1 11.3 %collective-permute-start.3 = (f32[3,24,1,8,128]{4,0,3,2,1:T(4,128)S(1)}, f32[3,24,1,8,128]{4,0,3,2,1:T(4,128)S(1)}, u32[]{:S(2)}, u32[]{:S(2)}) collective-permute-start(f32[3,24,1,8,128]{4,0,3,2,1:T(4,128)S(1)} %get-tuple-element.102), channel_id=1, source_target_pairs={{8,0},{16,8},{24,16},{32,24},{40,32},{48,40},{56,48},{64,56},{72,6... | collective-permute-start | bytes 884744 | tf_op jit(solution)/shard_map/ppermute | solution.py:28
  28.5 8.1 %collective-permute-start.4 = (f32[3,24,4,1,128]{4,0,3,2,1:T(4,128)S(1)}, f32[3,24,4,1,128]{4,0,3,2,1:T(4,128)S(1)}, u32[]{:S(2)}, u32[]{:S(2)}) collective-permute-start(f32[3,24,4,1,128]{4,0,3,2,1:T(4,128)S(1)} %get-tuple-element.79), channel_id=1, source_target_pairs={{0,1},{1,2},{2,3},{3,4},{4,5},{5,6},{6,7},{8,9},{9,10},{10,11},{11... | collective-permute-start | bytes 442376 | tf_op jit(solution)/shard_map/ppermute | solution.py:27
  32.7 11.3 %collective-permute-start.5 = (f32[3,24,4,1,128]{4,0,3,2,1:T(4,128)S(1)}, f32[3,24,4,1,128]{4,0,3,2,1:T(4,128)S(1)}, u32[]{:S(2)}, u32[]{:S(2)}) collective-permute-start(f32[3,24,4,1,128]{4,0,3,2,1:T(4,128)S(1)} %get-tuple-element.80), channel_id=1, source_target_pairs={{1,0},{2,1},{3,2},{4,3},{5,4},{6,5},{7,6},{9,8},{10,9},{11,10},{12... | collective-permute-start | bytes 442376 | tf_op jit(solution)/shard_map/ppermute | solution.py:28
  48.2 7.3 copy-start.1
  84.2 7.4 copy-start.12
  91.6 7.8 copy-start.2
  91.6 12.8 %slice-start = ((s8[5308416]{0:T(1024)(128)(4,1)}), s8[4194304]{0:T(1024)(128)(4,1)S(1)}, s32[]{:S(2)}) async-start(s8[5308416]{0:T(1024)(128)(4,1)} %bitcast.1303), calls=%async_computation | async-start | bytes 8388608
  142.9 9.4 %copy-start.10 = (f32[3,24,2,8,128]{4,3,2,1,0:T(8,128)S(1)}, f32[3,24,2,8,128]{4,3,2,1,0:T(8,128)}, u32[]{:S(2)}) copy-start(f32[3,24,2,8,128]{4,3,2,1,0:T(8,128)} %param.7) | copy-start | bytes 1769476
  516.3 22.4 %copy-start.11 = (f32[3,24,2,8,128]{4,0,3,2,1:T(4,128)S(1)}, f32[3,24,2,8,128]{4,0,3,2,1:T(4,128)}, u32[]{:S(2)}) copy-start(f32[3,24,2,8,128]{4,0,3,2,1:T(4,128)} %get-tuple-element.14) | copy-start | bytes 1769476
  518.3 11.5 %collective-permute-start.6 = (f32[3,24,1,8,128]{4,0,3,2,1:T(4,128)S(1)}, f32[3,24,1,8,128]{4,0,3,2,1:T(4,128)S(1)}, u32[]{:S(2)}, u32[]{:S(2)}) collective-permute-start(f32[3,24,1,8,128]{4,0,3,2,1:T(4,128)S(1)} %get-tuple-element.99), channel_id=1, source_target_pairs={{0,8},{8,16},{16,24},{24,32},{32,40},{40,48},{48,56},{56,64},{64,7... | collective-permute-start | bytes 884744 | tf_op jit(solution)/shard_map/ppermute | solution.py:27
  520.2 12.4 %collective-permute-start.7 = (f32[3,24,1,8,128]{4,0,3,2,1:T(4,128)S(1)}, f32[3,24,1,8,128]{4,0,3,2,1:T(4,128)S(1)}, u32[]{:S(2)}, u32[]{:S(2)}) collective-permute-start(f32[3,24,1,8,128]{4,0,3,2,1:T(4,128)S(1)} %get-tuple-element.100), channel_id=1, source_target_pairs={{8,0},{16,8},{24,16},{32,24},{40,32},{48,40},{56,48},{64,56},{72,6... | collective-permute-start | bytes 884744 | tf_op jit(solution)/shard_map/ppermute | solution.py:28
  532.8 7.5 collective-permute-start.8
  537.1 7.6 collective-permute-start.9
  548.8 7.3 copy-start
  745.4 7.1 collective-permute-start.10
  752.6 7.1 collective-permute-start.11
  765.6 5.1 copy-start.13
  770.8 7.6 collective-permute-start.13
  776.4 7.5 collective-permute-start.12
  783.9 5.3 collective-permute-start.14
  787.9 5.6 collective-permute-start.15
  (8 other events, 20.4 us)
